TPU v7x, 128 devices: a whole 4x4x4 slice. The times are simulated.
128 devices in a mesh: ctx: 8 (over x, z_lo), head: 16 (over z_hi, y, core).
Axes of the slice: x: 4, y: 4, z: 4 (z_hi: 2, z_lo: 2; z = z_hi * 2 + z_lo), core: 2. Of those that a mesh axis runs over, the one named last changes fastest.
Arguments:
- queries: bfloat16 [256, 16384], P(None, 'head'), may hold values from -64 to 64, as said below
- grad_out: bfloat16 [256, 16384], P(None, 'head'), may hold values from -24 to 24
- latent: bfloat16 [16384, 512], P(('ctx', 'head')), may hold values from -6.1 to 6.1
- up_key: bfloat16 [512, 16384], P(None, 'head'), as said below
- up_value: bfloat16 [512, 16384], P(None, 'head'), may hold values from -0.25 to 0.25
Outputs:
- grad_queries: float32 [256, 16384], P('ctx', 'head')
- grad_latent: float32 [16384, 512], P(('ctx', 'head'))
- grad_up_key: float32 [512, 16384], P('ctx', 'head')
- grad_up_value: float32 [512, 16384], P('ctx', 'head')
Inputs may be any that keep to these rules, and one draw needn't show every extreme that they name: `queries`: entries lie within 64 in magnitude. `up_key`: entries lie within 4 / sqrt(512) in magnitude.
All inputs are finite; a program needn't handle non-finite values.
Results may differ from a plain program's by a relative error of at most 0.005.
Values may be sent and summed in bfloat16 or wider, within the bound.
A program may use at most 128 MiB of HBM per device.

v0:
```python
import math

import jax
import jax.numpy as jnp
from jax import lax
from jax.sharding import PartitionSpec as P

HD = 128


def joined(part, axis, combine):
    gathered = jax.tree.map(lambda a: lax.all_gather(a, axis), part)

    def take(source):
        return jax.tree.map(lambda a: lax.dynamic_index_in_dim(a, source, 0, False), gathered)

    return lax.fori_loop(
        1, lax.axis_size(axis), lambda source, state: combine(state, take(source)), take(0)
    )


def join_pairs(former, latter):
    maxima = jnp.maximum(former[0], latter[0])
    left_factor = jnp.exp(former[0] - maxima)
    right_factor = jnp.exp(latter[0] - maxima)
    return (maxima, former[1] * left_factor + latter[1] * right_factor)


def local(queries, grad_out, latent, up_key, up_value):
    scale = 1.0 / math.sqrt(HD)
    local_heads = queries.shape[1] // HD
    width = queries.shape[1]
    query_count = queries.shape[0]
    contract_cols = (((1,), (1,)), ((), ()))
    contract_rows = (((0,), (0,)), ((), ()))
    block = lax.all_gather(latent, "head", axis=0, tiled=True)
    key_rows = block.shape[0]
    total_len = key_rows * lax.axis_size("ctx")
    first_key = lax.axis_index("ctx") * key_rows
    key_block = jnp.dot(block, up_key, preferred_element_type=jnp.float32)
    value_block = jnp.dot(block, up_value, preferred_element_type=jnp.float32).astype(jnp.bfloat16)
    query_pos = total_len - query_count + lax.iota(jnp.int32, query_count)
    key_pos = first_key + lax.iota(jnp.int32, key_rows)
    visible = key_pos[None, :] <= query_pos[:, None]
    head_ids = jnp.arange(local_heads, dtype=jnp.int32)

    def head_inputs(head_index):
        offset = head_index * HD
        return (
            lax.dynamic_slice_in_dim(queries, offset, HD, 1),
            lax.dynamic_slice_in_dim(grad_out, offset, HD, 1),
            lax.dynamic_slice_in_dim(key_block, offset, HD, 1),
            lax.dynamic_slice_in_dim(value_block, offset, HD, 1),
        )

    def masked_scores(query_head, key_head):
        raw = (
            lax.dot_general(
                query_head.astype(jnp.float32),
                key_head,
                contract_cols,
                precision=lax.Precision.HIGHEST,
            )
            * scale
        )
        return jnp.where(visible, raw, -jnp.inf)

    def product_scores(grad_head, value_head):
        return lax.dot_general(
            grad_head, value_head, contract_cols, preferred_element_type=jnp.float32
        )

    def pick_row(table, head_index):
        return lax.dynamic_index_in_dim(table, head_index, 0, keepdims=False)

    def local_pair(head_index):
        query_head, grad_head, key_head, value_head = head_inputs(head_index)
        scores = masked_scores(query_head, key_head)
        maxima = jnp.max(scores, axis=1)
        return (maxima, jnp.sum(jnp.exp(scores - maxima[:, None]), axis=1))

    local_max, local_sum = lax.map(local_pair, head_ids)
    maxima, totals = joined((local_max, local_sum), "ctx", join_pairs)

    def local_delta(head_index):
        query_head, grad_head, key_head, value_head = head_inputs(head_index)
        scores = masked_scores(query_head, key_head)
        probs = (
            jnp.exp(scores - pick_row(maxima, head_index)[:, None])
            / pick_row(totals, head_index)[:, None]
        )
        return jnp.sum(probs * product_scores(grad_head, value_head), axis=1)

    deltas = lax.psum(lax.map(local_delta, head_ids), "ctx")

    def accumulate(head_index, carry):
        query_acc, grad_kv = carry
        query_head, grad_head, key_head, value_head = head_inputs(head_index)
        scores = masked_scores(query_head, key_head)
        probs = (
            jnp.exp(scores - pick_row(maxima, head_index)[:, None])
            / pick_row(totals, head_index)[:, None]
        )
        grad_probs = product_scores(grad_head, value_head)
        grad_scores = (probs * (grad_probs - pick_row(deltas, head_index)[:, None]) * scale).astype(
            jnp.bfloat16
        )
        query_part = jnp.dot(
            grad_scores.astype(jnp.float32), key_head, precision=lax.Precision.HIGHEST
        )
        key_grad = lax.dot_general(
            grad_scores, query_head, contract_rows, preferred_element_type=jnp.float32
        ).astype(jnp.bfloat16)
        value_grad = lax.dot_general(
            probs.astype(jnp.bfloat16), grad_head, contract_rows, preferred_element_type=jnp.float32
        ).astype(jnp.bfloat16)
        offset = head_index * HD
        anchor = jnp.zeros((), jnp.int32)
        query_acc = lax.dynamic_update_slice(query_acc, query_part, (anchor, offset))
        grad_kv = lax.dynamic_update_slice(grad_kv, key_grad, (anchor, offset))
        grad_kv = lax.dynamic_update_slice(grad_kv, value_grad, (anchor, width + offset))
        return (query_acc, grad_kv)

    start_state = (
        jnp.zeros((query_count, width), jnp.float32),
        jnp.zeros((key_rows, 2 * width), jnp.bfloat16),
    )
    query_acc, grad_kv = lax.fori_loop(0, local_heads, accumulate, start_state)
    up_both = jnp.concatenate([up_key, up_value], axis=1)
    grad_queries = lax.psum_scatter(query_acc, "ctx", scatter_dimension=0, tiled=True)
    weight_sums = lax.psum_scatter(
        lax.dot_general(block, grad_kv, contract_rows, preferred_element_type=jnp.float32),
        "ctx",
        scatter_dimension=0,
        tiled=True,
    )
    own_rows = latent.shape[0]
    summed = lax.psum(
        lax.dot_general(grad_kv, up_both, contract_cols, preferred_element_type=jnp.float32), "head"
    )
    grad_latent = lax.dynamic_slice_in_dim(summed, lax.axis_index("head") * own_rows, own_rows, 0)
    return (grad_queries, grad_latent, weight_sums[:, :width], weight_sums[:, width:])


def solution(mesh):
    return jax.shard_map(
        local,
        mesh=mesh,
        in_specs=(
            P(None, "head"),
            P(None, "head"),
            P(("ctx", "head"), None),
            P(None, "head"),
            P(None, "head"),
        ),
        out_specs=(P("ctx", "head"), P(("ctx", "head"), None), P("ctx", "head"), P("ctx", "head")),
        check_vma=False,
    )
```

profile of v0, /device:TPU:1, one launch (start us, length us, event | category | flops | bytes accessed | tf_op | source)
XLA Modules:
  0.0 628.9 jit_solution(3696228629027708976)
XLA Ops:
  8.0 54.3 %all-gather.4.cloned.1.call-done = bf16[2048,512]{1,0:T(8,128)(2,1)} async-done(((bf16[128,512]{1,0:T(8,128)(2,1)}), bf16[2048,512]{1,0:T(8,128)(2,1)}) %all-gather.4.cloned.1.call-update) | async-done | bytes 2097168 | tf_op jit(solution)/shard_map/all_gather | solution.py:36
  62.3 7.4 %fusion.52 = f32[2048,1024]{1,0:T(8,128)} fusion(bf16[2048,512]{1,0:T(8,128)(2,1)} %all-gather.4.cloned.1.call-done, bf16[512,1024]{1,0:T(8,128)(2,1)} %param.16), kind=kOutput, calls=%fused_computation.71 | convolution fusion | flops 2147483648 | bytes 11534336 | tf_op jit(solution)/shard_map/dot_general | solution.py:40
  69.7 34.9 %while.60 = (s32[]{:T(128)}, f32[8,256]{1,0:T(8,128)S(1)}, f32[8,256]{1,0:T(8,128)S(1)}, s32[8]{0:T(128)S(1)}, bf16[256,1024]{1,0:T(8,128)(2,1)S(1)}, /*index=5*...) while((s32[]{:T(128)}, f32[8,256]{1,0:T(8,128)S(1)}, ...), condition=%wide.region_3.4_spmd.clone, body=%wide.region_0.3_spmd.clone.sunk | while | flops 808451584 | bytes 5326015 | solution.py:82
  71.0 2.5 fusion.85
  75.4 2.5 fusion.85
  79.8 2.5 fusion.85
  84.1 2.5 fusion.85
  88.5 2.5 fusion.85
  92.8 2.5 fusion.85
  97.2 2.5 fusion.85
  101.6 2.5 fusion.85
  104.6 21.8 %all-gather.1 = f32[64,256]{1,0:T(8,128)S(1)} all-gather(f32[8,256]{1,0:T(8,128)S(1)} %get-tuple-element.493), channel_id=3, replica_groups=mesh['ctx'=8,'head'=16] {'ctx'}, dimensions={0}, use_global_device_ids=true | all-gather | bytes 73728 | tf_op jit(solution)/shard_map/all_gather | solution.py:12
  126.5 21.8 %all-gather = f32[64,256]{1,0:T(8,128)S(1)} all-gather(f32[8,256]{1,0:T(8,128)S(1)} %get-tuple-element.492), channel_id=2, replica_groups=mesh['ctx'=8,'head'=16] {'ctx'}, dimensions={0}, use_global_device_ids=true | all-gather | bytes 73728 | tf_op jit(solution)/shard_map/all_gather | solution.py:12
  148.6 5.9 convolution_convert_fusion.2
  154.5 60.3 %while.61 = (s32[]{:T(128)}, f32[8,256]{1,0:T(8,128)S(1)}, s32[8]{0:T(128)S(1)}, bf16[256,1024]{1,0:T(8,128)(2,1)S(1)}, f32[2048,1024]{1,0:T(8,128)}, /*index=5*...) while((s32[]{:T(128)}, f32[8,256]{1,0:T(8,128)S(1)}, ...), condition=%wide.region_8.9_spmd.clone, body=%wide.region_6.8_spmd.clone.sunk | while | flops 943193856 | bytes 5918977 | solution.py:94
  157.7 2.7 fusion.90
  160.4 1.6 fusion.91
  165.2 2.7 fusion.90
  167.9 1.6 fusion.91
  172.8 2.7 fusion.90
  175.4 1.6 fusion.91
  180.3 2.7 fusion.90
  183.0 1.6 fusion.91
  187.9 2.7 fusion.90
  190.5 1.6 fusion.91
  195.4 2.7 fusion.90
  202.9 2.7 fusion.90
  210.5 2.7 fusion.90
  213.2 1.6 fusion.91
  214.8 15.7 %psum.14 = f32[8,256]{1,0:T(8,128)S(1)} all-reduce(f32[8,256]{1,0:T(8,128)S(1)} %get-tuple-element.496), channel_id=1, replica_groups=mesh['ctx'=8,'head'=16] {'ctx'}, use_global_device_ids=true, to_apply=%region_9.10 | all-reduce | flops 2048 | bytes 16384 | tf_op jit(solution)/shard_map/psum | solution.py:94
  230.7 4.3 broadcast_in_dim.48
  235.0 80.9 %while.62 = (s32[]{:T(128)}, f32[256,1024]{1,0:T(8,128)S(1)}, bf16[2048,2048]{1,0:T(8,128)(2,1)}, bf16[256,1024]{1,0:T(8,128)(2,1)S(1)}, f32[2048,1024]{1,0:T(8,...) while((s32[]{:T(128)}, f32[256,1024]{1,0:T(8,128)S(1)}, ...), condition=%wide.region_11.12_spmd.clone, body=%wide.region_10.11_spmd.clone.sunk | while | flops 2019033088 | bytes 13522222 | solution.py:128
  235.0 2.8 fusion.102
  239.3 2.3 convolution_dynamic-update-slice_fusion.2
  242.9 2.2 fusion.105
  245.2 2.7 fusion.102
  249.4 2.3 convolution_dynamic-update-slice_fusion.2
  253.0 2.2 fusion.105
  255.2 2.7 fusion.102
  259.5 2.3 convolution_dynamic-update-slice_fusion.2
  263.1 2.2 fusion.105
  265.4 2.7 fusion.102
  269.6 2.3 convolution_dynamic-update-slice_fusion.2
  273.2 2.2 fusion.105
  275.4 2.7 fusion.102
  279.7 2.3 convolution_dynamic-update-slice_fusion.2
  283.4 2.2 fusion.105
  285.6 2.7 fusion.102
  289.8 2.3 convolution_dynamic-update-slice_fusion.2
  293.4 2.2 fusion.105
  295.6 2.7 fusion.102
  299.9 2.3 convolution_dynamic-update-slice_fusion.2
  303.6 2.2 fusion.105
  305.7 2.7 fusion.102
  310.0 2.3 convolution_dynamic-update-slice_fusion.2
  313.6 2.2 fusion.105
  315.8 10.5 %fusion.45 = f32[2048,512]{1,0:T(8,128)} fusion(bf16[2048,2048]{1,0:T(8,128)(2,1)} %get-tuple-element.498, bf16[512,1024]{1,0:T(8,128)(2,1)} %param.17, bf16[512,1024]{1,0:T(8,128)(2,1)S(1)} %copy-done.3), kind=kOutput, calls=%fused_computation.61 | convolution fusion | flops 4299161600 | bytes 14680064 | tf_op jit(solution)/shard_map/dot_general | solution.py:139
  328.0 9.8 %convolution_bitcast_fusion = f32[512,2048]{0,1:T(8,128)} fusion(bf16[2048,2048]{1,0:T(8,128)(2,1)} %get-tuple-element.498, bf16[2048,512]{1,0:T(8,128)(2,1)S(1)} %copy-done.2), kind=kOutput, calls=%fused_computation.60 | convolution fusion | flops 4294967296 | bytes 14680064 | tf_op jit(solution)/shard_map/dot_general | solution.py:132
  337.7 5.4 copy.13
  343.8 145.6 %all-reduce.2.cloned.1.call-done = f32[2048,512]{1,0:T(8,128)} async-done(((f32[2048,512]{1,0:T(8,128)}), f32[2048,512]{1,0:T(8,128)}) %all-reduce.2.cloned.1.call-update) | async-done | bytes 4194320 | tf_op jit(solution)/shard_map/psum | solution.py:138
  489.4 1.7 constant_dynamic-slice_fusion.5
  491.0 92.3 %reduce-scatter.7.cloned.1.call-done = f32[64,2048]{1,0:T(8,128)} async-done(((f32[512,2048]{1,0:T(8,128)}), f32[64,2048]{1,0:T(8,128)}) %reduce-scatter.7.cloned.1.call-update) | async-done | bytes 524304
  583.4 1.9 fusion.51
  585.3 37.1 %reduce-scatter.5.cloned.1.call-done = f32[32,1024]{1,0:T(8,128)} async-done(((f32[256,1024]{1,0:T(8,128)}), f32[32,1024]{1,0:T(8,128)}) %reduce-scatter.5.cloned.1.call-update) | async-done | bytes 131088 | tf_op jit(solution)/shard_map/reduce_scatter | solution.py:130
  (126 shorter events, 44.4 us)
Async XLA Ops:
  7.2 55.1 %all-gather.4.cloned.1.call-start = ((), (), s32[]{:S(2)}) async-start(), calls=%async_computation.2 | async-start | bytes 2228224 | tf_op jit(solution)/shard_map/all_gather | solution.py:36
  7.9 481.5 %all-reduce.2.cloned.1.call-start = ((), (), s32[]{:S(2)}) async-start(), calls=%async_computation.4 | async-start | bytes 8388608 | tf_op jit(solution)/shard_map/psum | solution.py:138
  8.0 61.8 %copy-start.1 = (bf16[256,1024]{1,0:T(8,128)(2,1)S(1)}, bf16[256,1024]{1,0:T(8,128)(2,1)}, u32[]{:S(2)}) copy-start(bf16[256,1024]{1,0:T(8,128)(2,1)} %param.13) | copy-start | bytes 1572868
  69.7 78.9 %copy-start.4 = (bf16[512,1024]{1,0:T(8,128)(2,1)S(1)}, bf16[512,1024]{1,0:T(8,128)(2,1)}, u32[]{:S(2)}) copy-start(bf16[512,1024]{1,0:T(8,128)(2,1)} %param.17) | copy-start | bytes 3145732
  235.0 80.9 %copy-start.3 = (bf16[512,1024]{1,0:T(8,128)(2,1)S(1)}, bf16[512,1024]{1,0:T(8,128)(2,1)}, u32[]{:S(2)}) copy-start(bf16[512,1024]{1,0:T(8,128)(2,1)} %param.16) | copy-start | bytes 3145732
  315.8 10.5 %copy-start = (f32[256,1024]{1,0:T(8,128)}, f32[256,1024]{1,0:T(8,128)S(1)}, u32[]{:S(2)}) copy-start(f32[256,1024]{1,0:T(8,128)S(1)} %get-tuple-element.497) | copy-start | bytes 3145732
  326.4 1.6 copy-start.2
  326.4 257.0 %reduce-scatter.7.cloned.1.call-start = ((), (), s32[]{:S(2)}) async-start(), calls=%async_computation.5 | async-start | bytes 4718592
  343.2 279.1 %reduce-scatter.5.cloned.1.call-start = ((), (), s32[]{:S(2)}) async-start(), calls=%async_computation.3 | async-start | bytes 1179648 | tf_op jit(solution)/shard_map/reduce_scatter | solution.py:130
Sparse Core Ops, SparseCore 0:
  10.4 51.8 all-gather.3
  326.5 162.8 all-reduce.1
  491.8 91.5 reduce-scatter.6
  586.2 36.0 reduce-scatter.4
where the time goes:
time: 636 us; the launch traced here: 629 us
  waiting for transfers between devices  331 us (52%)
  matrix products  169 us (27%)
  blocking collectives  59.4 us (9%)
  loops' own time  26.7 us (4%)
  local copies, waits for them, and re-layouts  25.9 us (4%)
  between operations  13.9 us (2%)
    psum x1, waiting for transfers between devices, local(): lax.psum(lax.dot_general(grad_kv, up_both, contract_cols, preferred_eleme...  146 us
    unnamed x5, waiting for transfers between devices  93.6 us
    dot_general x24, matrix products, masked_scores(): lax.dot_general(query_head.astype(jnp.float32), key_head, contract_cols,...  63.4 us
    all_gather x1, waiting for transfers between devices, local(): block = lax.all_gather(latent, 'head', axis=0, tiled=True)  54.3 us
    all_gather x2, blocking collectives, joined(): gathered = jax.tree.map(lambda a: lax.all_gather(a, axis), part)  43.6 us
    reduce_scatter x1, waiting for transfers between devices, local(): lax.psum_scatter(query_acc, 'ctx', scatter_dimension=0, tiled=True)  37.1 us
    dot_general x16, matrix products, product_scores(): lax.dot_general(grad_head, value_head, contract_cols, preferred_element_t...  25.1 us
    another operation x1, loops' own time, local(): deltas = lax.psum(lax.map(local_delta, head_ids), 'ctx')  21 us
  transfers between devices with their start and end apart: 4, of which 4 were waited for; matrix products, arithmetic and copies ran while one was open for 3% of the time, Pallas kernels for 0%

commit v1 on v0

v1 whole, which is shorter than its diff:
```python
import math

import jax
import jax.numpy as jnp
from jax import lax
from jax.experimental import pallas as pl
from jax.experimental.pallas import tpu as pltpu
from jax.sharding import PartitionSpec as P

HD = 128
NH = 8
ROWS = 2048
TILE = 256
NQ = 256
NEG = -1e30
F32 = jnp.float32
BF16 = jnp.bfloat16
MESH = pl.DeviceIdType.MESH
SCALE = 1.0 / math.sqrt(HD)
TN = (((0,), (0,)), ((), ()))


def dot(a, b):
    return jnp.dot(a, b, preferred_element_type=F32)


def kernel(
    q_ref, go_ref, own_ref, upk_ref, upv_ref,
    gq_out, gl_out, gk_out, gv_out,
    lat, lat_t, up_t, q_t, go_t, kk, ebuf, gbuf, bias,
    mst, tst, dst, st_all, wst, delta, acc,
    pbuf, r1, rd, r2, rz, zs, fsum,
    gds, gdr, ys, yr, lzs, lzr,
    ag_send, ag_recv, st_send, st_recv,
    s1_send, s1_recv, sd_send, sd_recv, s2_send, s2_recv, sz_send, sz_recv,
    gd_send, gd_recv, y_send, y_recv, lz_send, lz_recv,
):
    ci = lax.axis_index("ctx")
    hi = lax.axis_index("head")
    x, zl = ci // 2, ci % 2
    zh, y, core = hi // 8, (hi // 2) % 4, hi % 2
    oz = 1 - zh

    def ym(d):
        return (y + d) % 4

    def xm(d):
        return (x + d) % 4

    partner = (ci, zh * 8 + y * 2 + 1 - core)
    ydev = {s: (ci, zh * 8 + ym(s) * 2 + core) for s in (1, 3)}
    zdev = (x * 2 + 1 - zl, oz * 8 + y * 2 + core)
    xdev = {s: (xm(s) * 2 + zl, hi) for s in (1, 3)}
    rdev = (x * 2 + 1 - zl, hi)
    peers = [((ci + d) % 8, hi) for d in range(1, 8)]

    barrier = pltpu.get_barrier_semaphore()
    for d in [partner, ydev[1], ydev[3], zdev] + peers:
        pl.semaphore_signal(barrier, inc=1, device_id=d, device_id_type=MESH)

    def remote(src, dst, ss, rs, device):
        return pltpu.make_async_remote_copy(
            src_ref=src, dst_ref=dst, send_sem=ss, recv_sem=rs,
            device_id=device, device_id_type=MESH,
        )

    def slot(z_, y_, c_):
        return z_ * 8 + y_ * 2 + c_

    def ag(index, s, device, src=None):
        rows = lat.at[pl.ds(pl.multiple_of(s * 128, 128), 128), :]
        return remote(rows if src is None else src, rows, ag_send.at[index], ag_recv.at[s], device)

    s_o, s_z = slot(zh, y, core), slot(oz, y, core)
    s_l, s_lz = slot(zh, ym(3), core), slot(oz, ym(3), core)
    s_r, s_rz = slot(zh, ym(1), core), slot(oz, ym(1), core)
    s_f, s_fz = slot(zh, ym(2), core), slot(oz, ym(2), core)
    arrivals = {
        0: (s_o, ((0, zdev), (1, ydev[1]), (2, ydev[3]), (3, partner))),
        1: (s_z, ((4, ydev[1]), (5, ydev[3]), (6, partner))),
        2: (s_l, ((7, ydev[1]), (8, partner))),
        3: (s_lz, ((10, partner),)),
        4: (s_r, ((9, partner),)),
        5: (s_rz, ((11, ydev[3]), (12, partner))),
        6: (s_f, ((13, partner),)),
        7: (s_fz, ((14, partner),)),
    }
    other = {
        k: s + 1 - 2 * core for k, (s, _) in arrivals.items()
    }

    def arrive(k):
        s, sends = arrivals[k]
        ag(sends[0][0], s, partner).wait_recv()
        for index, device in sends:
            ag(index, s, device).start()

    lat[pl.ds(pl.multiple_of(s_o * 128, 128), 128), :] = own_ref[...]
    pl.semaphore_wait(barrier, 11)
    for index, device in arrivals[0][1]:
        ag(index, s_o, device, own_ref).start()

    for h in range(NH):
        cols = slice(h * HD, (h + 1) * HD)
        q_t[h] = q_ref[:, cols].T
        go_t[h] = go_ref[:, cols].T

    @pl.loop(0, NH)
    def _(h):
        cols = pl.ds(pl.multiple_of(h * HD, HD), HD)
        rows = pl.multiple_of(h * 2 * HD, 2 * HD)
        up_t[pl.ds(rows, HD), :] = upk_ref[:, cols].T
        up_t[pl.ds(rows + HD, HD), :] = upv_ref[:, cols].T

    last_owner = jnp.logical_and(x == 3, zl == zh)
    key_row = lax.broadcasted_iota(jnp.int32, (TILE, NQ), 0)
    query_col = lax.broadcasted_iota(jnp.int32, (TILE, NQ), 1)

    @pl.loop(0, 8)
    def _(step):
        for k in range(1, 8):
            @pl.when(step == max(k - 1, 1))
            def _(k=k):
                arrive(k)
        for k in range(8):
            @pl.when(step == k)
            def _(k=k):
                ag(arrivals[k][1][0][0], other[k], partner).wait_recv()
        v = (3 * (step // 2)) % 5
        y_t = (y + v - 2 * (v // 4)) % 4
        z_t = (zh + step % 2) % 2
        t = z_t * 4 + y_t
        rows = pl.ds(pl.multiple_of(t * TILE, TILE), TILE)
        limit = jnp.where(jnp.logical_and(last_owner, t == 7), 0, 4 * TILE)
        bias[...] = jnp.where(key_row > query_col + limit, NEG, 0.0)
        block = lat[rows, :]
        lat_t[:, rows] = block.T
        for pair in range(NH // 2):
            cols = slice(pair * 2 * HD, (pair + 1) * 2 * HD)
            k2 = dot(block, upk_ref[:, cols])
            v2 = dot(block, upv_ref[:, cols]).astype(BF16)
            for b in range(2):
                h = pair * 2 + b
                half = slice(b * HD, (b + 1) * HD)
                key = k2[:, half]
                key_hi = key.astype(BF16)
                key_lo = (key - key_hi.astype(F32)).astype(BF16)
                both = jnp.concatenate([key_hi, key_lo], axis=1)
                kk[rows, h * 256:(h + 1) * 256] = both
                qt = q_t[h]
                s = dot(both, jnp.concatenate([qt, qt], axis=0)) + bias[...]
                g = dot(v2[:, half], go_t[h])
                m = jnp.max(s, axis=0, keepdims=True)
                e = jnp.exp((s - m) * SCALE)
                ebuf[h, rows, :] = e
                gbuf[h, rows, :] = g
                mst[h, pl.ds(t, 1), :] = m
                tst[h, pl.ds(t, 1), :] = jnp.sum(e, axis=0, keepdims=True)
                dst[h, pl.ds(t, 1), :] = jnp.sum(e * g, axis=0, keepdims=True)

    for h in range(NH):
        mt = mst[h]
        m = jnp.max(mt, axis=0, keepdims=True)
        w = jnp.exp((mt - m) * SCALE)
        st_all[ci, h:h + 1, :] = m
        st_all[ci, NH + h:NH + h + 1, :] = jnp.sum(w * tst[h], axis=0, keepdims=True)
        st_all[ci, 2 * NH + h:2 * NH + h + 1, :] = jnp.sum(w * dst[h], axis=0, keepdims=True)

    def stat(d, index):
        return remote(st_all.at[index], st_all.at[index], st_send.at[d - 1], st_recv.at[index], peers[d - 1])

    for d in range(1, 8):
        stat(d, ci).start()
    for d in range(1, 8):
        stat(d, (ci + d) % 8).wait_recv()
    m_all = st_all[0, 0:NH, :]
    for c in range(1, 8):
        m_all = jnp.maximum(m_all, st_all[c, 0:NH, :])
    total = jnp.zeros((NH, NQ), F32)
    product = jnp.zeros((NH, NQ), F32)
    for c in range(8):
        w = jnp.exp((st_all[c, 0:NH, :] - m_all) * SCALE)
        total += w * st_all[c, NH:2 * NH, :]
        product += w * st_all[c, 2 * NH:3 * NH, :]
    delta[...] = product / total
    inverse = 1.0 / total
    for h in range(NH):
        wst[h] = jnp.exp((mst[h] - m_all[h:h + 1]) * SCALE) * inverse[h:h + 1]

    def stage1(h, s):
        return remote(pbuf.at[h, xm(2)], r1.at[h], s1_send.at[h], s1_recv.at[h], xdev[s])

    def direct(h, s):
        return remote(pbuf.at[h, xm(-s)], rd.at[h], sd_send.at[h], sd_recv.at[h], xdev[4 - s])

    def stage2(h, s):
        return remote(pbuf.at[h, xm(s)], r2.at[h], s2_send.at[h], s2_recv.at[h], xdev[s])

    def stagez(h):
        return remote(zs.at[h], rz.at[h], sz_send.at[h], sz_recv.at[h], rdev)

    def up_relay(h, s):
        stage1(h, s).wait_recv()
        pbuf[h, xm(s)] = (pbuf[h, xm(s)].astype(F32) + r1[h].astype(F32)).astype(BF16)
        stage2(h, s).start()

    def up_join(h, s):
        direct(h, s).wait_recv()
        stage2(h, s).wait_recv()

        def part(z_):
            return pbuf[h, x, z_].astype(F32) + rd[h, z_].astype(F32) + r2[h, z_].astype(F32)

        zs[h] = part(1 - zl).astype(BF16)
        stagez(h).start()
        fsum[h] = part(zl)

    @pl.loop(0, NH // 2)
    def _(hp):
        qcols = pl.ds(pl.multiple_of(hp * 2 * HD, 2 * HD), 2 * HD)
        q2 = q_ref[:, qcols]
        go2 = go_ref[:, qcols]
        acc[...] = jnp.zeros_like(acc)

        @pl.loop(0, 8)
        def _(t):
            rows = pl.ds(pl.multiple_of(t * TILE, TILE), TILE)
            for b in range(2):
                h = hp * 2 + b
                kcols = pl.ds(pl.multiple_of(h * 256, 256), 256)
                e = ebuf[h, rows, :]
                w = wst[h, pl.ds(t, 1), :]
                prob = e * w
                gs = (prob * (gbuf[h, rows, :] - delta[pl.ds(h, 1), :]) * SCALE).astype(BF16)
                acc[b] += lax.dot_general(gs, kk[rows, kcols], TN, preferred_element_type=F32)
                half = slice(b * HD, (b + 1) * HD)
                gk = dot(gs, q2[:, half]).astype(BF16)
                gv = dot(prob.astype(BF16), go2[:, half]).astype(BF16)
                kk[rows, kcols] = jnp.concatenate([gk, gv], axis=1)

        for b in range(2):
            h = hp * 2 + b
            s = 1 if b == 0 else 3
            kcols = pl.ds(pl.multiple_of(h * 256, 256), 256)
            gq = acc[b, :, 0:HD] + acc[b, :, HD:2 * HD]
            up = dot(lat_t[...], kk[:, kcols]).astype(BF16)
            for x_ in range(4):
                for z_ in range(2):
                    first = x_ * 128 + z_ * 64
                    pbuf[h, x_, z_, 0:64, :] = up[first:first + 64, :]
                    first = x_ * 64 + z_ * 32
                    pbuf[h, x_, z_, 64:80, :] = jnp.concatenate(
                        [gq[first:first + 16], gq[first + 16:first + 32]], axis=1
                    ).astype(BF16)
            stage1(h, s).start()
            direct(h, s).start()

        @pl.when(hp >= 1)
        def _():
            up_relay(hp * 2 - 2, 1)
            up_relay(hp * 2 - 1, 3)

        @pl.when(hp >= 2)
        def _():
            up_join(hp * 2 - 4, 1)
            up_join(hp * 2 - 3, 3)

    def pairwise(d):
        return remote(gds.at[d], gdr.at[d], gd_send.at[d], gd_recv.at[d], partner)

    def latent_part(d):
        y_ = ym(d)
        for z_ in range(2):
            first = pl.multiple_of((z_ * 4 + y_) * TILE, TILE)
            part = dot(kk[pl.ds(first, TILE), :], up_t[...])
            acc[0] = part[:, 0:256]
            acc[1] = part[:, 256:512]
            mine = pl.ds(pl.multiple_of(core * 128, 128), 128)
            theirs = pl.ds(pl.multiple_of((1 - core) * 128, 128), 128)
            for b in range(2):
                ebuf[b, pl.ds(d * 256 + z_ * 128, 128), :] = acc[b, mine, :]
                gds[d, b, z_] = acc[b, theirs, :].astype(BF16)
        pairwise(d).start()

    def held(d, b):
        pieces = []
        for z_ in range(2):
            pieces.append(ebuf[b, pl.ds(d * 256 + z_ * 128, 128), :] + gdr[d, b, z_].astype(F32))
        return pieces

    def ycopy(b, kind, s):
        return remote(ys.at[b, kind], yr.at[b, kind], y_send.at[b, kind], y_recv.at[b, kind], ydev[s])

    def ysend(b, kind, s, pieces):
        for z_ in range(2):
            ys[b, kind, z_] = pieces[z_].astype(BF16)
        ycopy(b, kind, s).start()

    DIRS = ((0, 1), (1, 3))
    latent_part(2)
    up_relay(6, 1)
    up_relay(7, 3)
    latent_part(1)
    pairwise(2).wait_recv()
    for b, s in DIRS:
        ysend(b, 0, s, held(2, b))
    latent_part(3)
    up_join(4, 1)
    up_join(5, 3)
    pairwise(1).wait_recv()
    pairwise(3).wait_recv()
    for b, s in DIRS:
        ysend(b, 1, 4 - s, held(4 - s, b))
    latent_part(0)
    for b, s in DIRS:
        ycopy(b, 0, s).wait_recv()
        pieces = held(s, b)
        ysend(b, 2, s, [pieces[z_] + yr[b, 0, z_].astype(F32) for z_ in range(2)])
    up_join(6, 1)
    up_join(7, 3)
    pairwise(0).wait_recv()
    for b, s in DIRS:
        ycopy(b, 1, 4 - s).wait_recv()
        ycopy(b, 2, s).wait_recv()
        pieces = held(0, b)
        for z_ in range(2):
            total_piece = pieces[z_] + yr[b, 1, z_].astype(F32) + yr[b, 2, z_].astype(F32)
            acc[b, z_ * 128:(z_ + 1) * 128, :] = total_piece
        lzs[b] = acc[b, pl.ds(pl.multiple_of(oz * 128, 128), 128), :].astype(BF16)
        remote(lzs.at[b], lzr.at[b], lz_send.at[b], lz_recv.at[b], zdev).start()
    for h in range(NH):
        stagez(h).wait_recv()
        out = fsum[h] + rz[h].astype(F32)
        cols = slice(h * HD, (h + 1) * HD)
        gk_out[:, cols] = out[0:64, 0:HD]
        gv_out[:, cols] = out[0:64, HD:2 * HD]
        gq_out[0:16, cols] = out[64:80, 0:HD]
        gq_out[16:32, cols] = out[64:80, HD:2 * HD]
    for b in range(2):
        copy = remote(lzs.at[b], lzr.at[b], lz_send.at[b], lz_recv.at[b], zdev)
        copy.wait_recv()
        mine = pl.ds(pl.multiple_of(zh * 128, 128), 128)
        gl_out[:, b * 256:(b + 1) * 256] = acc[b, mine, :] + lzr[b].astype(F32)
        copy.wait_send()

    for k in range(8):
        for index, device in arrivals[k][1]:
            ag(index, arrivals[k][0], device, own_ref if k == 0 else None).wait_send()
    for d in range(1, 8):
        stat(d, ci).wait_send()
    for h in range(NH):
        s = 1 if h % 2 == 0 else 3
        stage1(h, s).wait_send()
        direct(h, s).wait_send()
        stage2(h, s).wait_send()
        stagez(h).wait_send()
    for d in range(4):
        pairwise(d).wait_send()
    for b, s in DIRS:
        ycopy(b, 0, s).wait_send()
        ycopy(b, 1, 4 - s).wait_send()
        ycopy(b, 2, s).wait_send()


def local(queries, grad_out, latent, up_key, up_value):
    dma = pltpu.SemaphoreType.DMA
    vmem = pltpu.VMEM
    full = pl.BlockSpec(memory_space=pltpu.VMEM)
    shape = jax.ShapeDtypeStruct
    return pl.pallas_call(
        kernel,
        out_shape=(
            shape((32, 1024), F32), shape((128, 512), F32),
            shape((64, 1024), F32), shape((64, 1024), F32),
        ),
        in_specs=[full] * 5,
        out_specs=(full,) * 4,
        scratch_shapes=[
            vmem((ROWS, 512), BF16), vmem((512, ROWS), BF16), vmem((2048, 512), BF16),
            vmem((NH, HD, NQ), BF16), vmem((NH, HD, NQ), BF16),
            vmem((ROWS, 2048), BF16), vmem((NH, ROWS, NQ), F32), vmem((NH, ROWS, NQ), F32),
            vmem((TILE, NQ), F32),
            vmem((NH, 8, NQ), F32), vmem((NH, 8, NQ), F32), vmem((NH, 8, NQ), F32),
            vmem((8, 3 * NH, NQ), F32), vmem((NH, 8, NQ), F32), vmem((NH, NQ), F32),
            vmem((2, 256, 256), F32),
            vmem((NH, 4, 2, 80, 256), BF16),
            vmem((NH, 2, 80, 256), BF16), vmem((NH, 2, 80, 256), BF16), vmem((NH, 2, 80, 256), BF16),
            vmem((NH, 80, 256), BF16), vmem((NH, 80, 256), BF16), vmem((NH, 80, 256), F32),
            vmem((4, 2, 2, 128, 256), BF16), vmem((4, 2, 2, 128, 256), BF16),
            vmem((2, 3, 2, 128, 256), BF16), vmem((2, 3, 2, 128, 256), BF16),
            vmem((2, 128, 256), BF16), vmem((2, 128, 256), BF16),
            dma((15,)), dma((16,)), dma((7,)), dma((8,)),
            dma((NH,)), dma((NH,)), dma((NH,)), dma((NH,)),
            dma((NH,)), dma((NH,)), dma((NH,)), dma((NH,)),
            dma((4,)), dma((4,)), dma((2, 3)), dma((2, 3)), dma((2,)), dma((2,)),
        ],
        compiler_params=pltpu.CompilerParams(
            collective_id=0, has_side_effects=True, vmem_limit_bytes=67043328
        ),
    )(queries, grad_out, latent, up_key, up_value)


def solution(mesh):
    return jax.shard_map(
        local,
        mesh=mesh,
        in_specs=(
            P(None, "head"),
            P(None, "head"),
            P(("ctx", "head"), None),
            P(None, "head"),
            P(None, "head"),
        ),
        out_specs=(P("ctx", "head"), P(("ctx", "head"), None), P("ctx", "head"), P("ctx", "head")),
        check_vma=False,
    )
```

time: 636 us -> 93.2 us (0.15); the launches traced: 629 us -> 93 us
  waiting for transfers between devices: 331 us -> 0 us
  matrix products: 169 us -> 0 us
  Pallas kernels: 0 us -> 87.9 us
  blocking collectives: 59.4 us -> 0 us
  loops' own time: 26.7 us -> 0 us
  local copies, waits for them, and re-layouts: 25.9 us -> 4.4 us
  between operations: 13.9 us -> 0.65 us
    dot_general x68 -> x0, matrix products: 169 us -> none  [the longest x24 63.4 us: masked_scores(): lax.dot_general(query_head.astype(jnp.float32), key_head, contract_cols,...]
    psum x1 -> x0, waiting for transfers between devices: 146 us -> none  [local(): lax.psum(lax.dot_general(grad_kv, up_both, contract_cols, preferred_eleme...]
    unnamed x5 -> x0, waiting for transfers between devices: 93.6 us -> none
    pallas_call x0 -> x1, Pallas kernels: none -> 87.9 us  [local(): pl.pallas_call(kernel, out_shape=(shape((32, 1024), F32), shape((128, 512...]
    all_gather x1 -> x0, waiting for transfers between devices: 54.3 us -> none  [local(): block = lax.all_gather(latent, 'head', axis=0, tiled=True)]
    all_gather x2 -> x0, blocking collectives: 43.6 us -> none  [joined(): gathered = jax.tree.map(lambda a: lax.all_gather(a, axis), part)]
    reduce_scatter x1 -> x0, waiting for transfers between devices: 37.1 us -> none  [local(): lax.psum_scatter(query_acc, 'ctx', scatter_dimension=0, tiled=True)]
    another operation x4 -> x0, loops' own time: 26.7 us -> none  [the longest x1 21 us: local(): deltas = lax.psum(lax.map(local_delta, head_ids), 'ctx')]
  transfers between devices with their start and end apart: 4 -> 0, of which waited for: 4 -> 0; matrix products, arithmetic and copies ran while one was open for 3% -> 0% of each run, Pallas kernels for 0% -> 0%
where the time goes in v1:
time: 93.2 us; the launch traced here: 93 us
  Pallas kernels  87.9 us (94%)
  local copies, waits for them, and re-layouts  4.4 us (5%)
    pallas_call x1, Pallas kernels, local(): pl.pallas_call(kernel, out_shape=(shape((32, 1024), F32), shape((128, 512...  87.9 us
    unnamed x10, local copies, waits for them, and re-layouts  4.4 us

profile of v1, /device:TPU:1, one launch (start us, length us, event | category | flops | bytes accessed | tf_op | source)
XLA Modules:
  0.0 93.0 jit_solution(10316844480651896038)
XLA Ops:
  0.6 87.9 %shard_map.84 = (f32[32,1024]{1,0:T(8,128)}, f32[128,512]{1,0:T(8,128)}, f32[64,1024]{1,0:T(8,128)}, f32[64,1024]{1,0:T(8,128)}) custom-call(bf16[256,1024]{1,0:T(8,128)(2,1)} %q_ref.1, bf16[256,1024]{1,0:T(8,128)(2,1)} %go_ref.1, bf16[128,512]{1,0:T(8,128)(2,1)} %own_ref.1, bf16[512,1024]{1,0:T(8,128)(2,1)} %upk_ref.1, bf16[512,1024]{1,0:T(8,128)(2,1)} %upv_ref.1), custom_call_target="tpu_custom_call" | custom-call | tf_op jit(solution)/shard_map/pallas_call | solution.py:370
  88.6 0.0 copy-start.2
  88.6 1.6 %copy.13 = f32[32,1024]{1,0:T(8,128)} copy(f32[32,1024]{1,0:T(8,128)} %get-tuple-element.8) | data formatting | bytes 262144
  90.2 0.0 copy-done.2
  90.2 0.0 copy-start.1
  90.2 0.7 copy.14
  90.9 0.3 copy-done.1
  91.2 0.0 copy-start
  91.2 0.7 copy.15
  91.9 0.3 copy-done
  92.3 0.7 copy.16
Async XLA Ops:
  88.6 1.6 %copy-start.2 = (f32[128,512]{1,0:T(8,128)S(1)}, f32[128,512]{1,0:T(8,128)}, u32[]{:S(2)}) copy-start(f32[128,512]{1,0:T(8,128)} %get-tuple-element.9) | copy-start | bytes 786436
  90.2 1.0 %copy-start.1 = (f32[64,1024]{1,0:T(8,128)S(1)}, f32[64,1024]{1,0:T(8,128)}, u32[]{:S(2)}) copy-start(f32[64,1024]{1,0:T(8,128)} %get-tuple-element.10) | copy-start | bytes 786436
  91.2 1.0 %copy-start = (f32[64,1024]{1,0:T(8,128)S(1)}, f32[64,1024]{1,0:T(8,128)}, u32[]{:S(2)}) copy-start(f32[64,1024]{1,0:T(8,128)} %get-tuple-element.11) | copy-start | bytes 786436

commit v2 on v1

v2 whole, which is shorter than its diff:
```python
import math

import jax
import jax.numpy as jnp
from jax import lax
from jax.experimental import pallas as pl
from jax.experimental.pallas import tpu as pltpu
from jax.sharding import PartitionSpec as P

HD = 128
NH = 8
ROWS = 2048
TILE = 256
NQ = 256
NEG = -1e30
F32 = jnp.float32
BF16 = jnp.bfloat16
MESH = pl.DeviceIdType.MESH
SCALE = 1.0 / math.sqrt(HD)
SCALE2 = SCALE / math.log(2.0)
TN = (((0,), (0,)), ((), ()))


def dot(a, b):
    return jnp.dot(a, b, preferred_element_type=F32)


def kernel(
    q_hbm, go_hbm, own_hbm, upk_hbm, upv_hbm,
    gq_out, gl_out, gk_out, gv_out,
    q_ref, go_ref, upk_ref, upv_ref,
    lat, lat_t, up_t, q_t, go_t, kk, ebuf, gbuf, bias,
    mst, tst, dst, st_all, wst, delta, acc,
    pbuf, rbuf, gds, gdr, ls, lr, held, lpart,
    in_sem, ag_send, ag_recv, st_send, st_recv, up_send, up_recv,
    gd_send, gd_recv, l_send, l_recv,
):
    ci = lax.axis_index("ctx")
    hi = lax.axis_index("head")
    x, zl = ci // 2, ci % 2
    zh, y, core = hi // 8, (hi // 2) % 4, hi % 2
    oz = 1 - zh

    def ym(d):
        return (y + d) % 4

    def xm(d):
        return (x + d) % 4

    partner = (ci, zh * 8 + y * 2 + 1 - core)
    peers = [((ci + d) % 8, hi) for d in range(1, 8)]

    def chip(z_, d):
        if z_ == 0:
            return (ci, zh * 8 + ym(d) * 2 + core)
        return (x * 2 + 1 - zl, oz * 8 + ym(d) * 2 + core)

    def slot(z_, y_, c_):
        return z_ * 8 + y_ * 2 + c_

    def slot_rows(s):
        return lat.at[pl.ds(pl.multiple_of(s * 128, 128), 128), :]

    own_slot = slot(zh, y, core)
    loads = [
        pltpu.make_async_copy(src, dst, in_sem.at[i])
        for i, (src, dst) in enumerate((
            (own_hbm, slot_rows(own_slot)), (q_hbm, q_ref), (go_hbm, go_ref),
            (upk_hbm, upk_ref), (upv_hbm, upv_ref),
        ))
    ]
    for load in loads:
        load.start()

    order = ((1, 0), (0, 3), (0, 1), (1, 3), (1, 1), (0, 2), (1, 2))
    barrier = pltpu.get_barrier_semaphore()
    for d in [partner] + [chip(z_, d) for z_, d in order] + peers:
        pl.semaphore_signal(barrier, inc=1, device_id=d, device_id_type=MESH)

    def remote(src, dst, ss, rs, device):
        return pltpu.make_async_remote_copy(
            src_ref=src, dst_ref=dst, send_sem=ss, recv_sem=rs,
            device_id=device, device_id_type=MESH,
        )

    def ag(index, s, device):
        return remote(slot_rows(s), slot_rows(s), ag_send.at[index], ag_recv.at[s], device)

    slots = [own_slot] + [slot(zh if z_ == 0 else oz, ym(d), core) for z_, d in order]

    def outgoing(k):
        z_, d = order[k - 1]
        return ag(k, own_slot, chip(z_, (4 - d) % 4))

    def forward(k):
        return ag(7 + k, slots[k], partner)

    loads[0].wait()
    pl.semaphore_wait(barrier, 15)
    ag(0, own_slot, partner).start()
    for k in range(1, 4):
        outgoing(k).start()
    for load in loads[1:]:
        load.wait()

    for h in range(NH):
        cols = slice(h * HD, (h + 1) * HD)
        q_t[h] = q_ref[:, cols].T
        go_t[h] = go_ref[:, cols].T

    last_owner = jnp.logical_and(x == 3, zl == zh)
    key_row = lax.broadcasted_iota(jnp.int32, (TILE, NQ), 0)
    query_col = lax.broadcasted_iota(jnp.int32, (TILE, NQ), 1)

    @pl.loop(0, 8)
    def _(step):
        @pl.when(step == 1)
        def _():
            outgoing(4).start()
            outgoing(5).start()

        for k in range(1, 8):
            @pl.when(step == max(k - 1, 1))
            def _(k=k):
                ag(k, slots[k], partner).wait_recv()
                forward(k).start()
                if k == 1:
                    outgoing(6).start()
                    outgoing(7).start()
        for k in range(8):
            @pl.when(step == k)
            def _(k=k):
                ag(0, slots[k] + 1 - 2 * core, partner).wait_recv()
        y_t = (y + jnp.where(step < 2, 0, jnp.where(step >= 6, 2, jnp.where(step % 2 == 0, 3, 1)))) % 4
        z_t = (zh + jnp.where(step < 4, jnp.where(step == 1, 1, 0), jnp.where(step == 6, 0, 1))) % 2
        t = z_t * 4 + y_t
        rows = pl.ds(pl.multiple_of(t * TILE, TILE), TILE)
        limit = jnp.where(jnp.logical_and(last_owner, t == 7), 0, 4 * TILE)
        bias[...] = jnp.where(key_row > query_col + limit, NEG, 0.0)
        block = lat[rows, :]
        lat_t[:, rows] = block.T
        for pair in range(NH // 2):
            cols = slice(pair * 2 * HD, (pair + 1) * 2 * HD)
            k2 = dot(block, upk_ref[:, cols])
            v2 = dot(block, upv_ref[:, cols]).astype(BF16)
            for b in range(2):
                h = pair * 2 + b
                half = slice(b * HD, (b + 1) * HD)
                key = k2[:, half]
                key_hi = key.astype(BF16)
                key_lo = (key - key_hi.astype(F32)).astype(BF16)
                both = jnp.concatenate([key_hi, key_lo], axis=1)
                kk[rows, h * 256:(h + 1) * 256] = both
                qt = q_t[h]
                s = dot(both, jnp.concatenate([qt, qt], axis=0)) + bias[...]
                g = dot(v2[:, half], go_t[h])
                m = jnp.max(s, axis=0, keepdims=True)
                e = jnp.exp2((s - m) * SCALE2)
                ebuf[h, rows, :] = e
                gbuf[h, rows, :] = g
                mst[h, pl.ds(t, 1), :] = m
                tst[h, pl.ds(t, 1), :] = jnp.sum(e, axis=0, keepdims=True)
                dst[h, pl.ds(t, 1), :] = jnp.sum(e * g, axis=0, keepdims=True)

    for h in range(NH):
        mt = mst[h]
        m = jnp.max(mt, axis=0, keepdims=True)
        w = jnp.exp2((mt - m) * SCALE2)
        st_all[ci, h:h + 1, :] = m
        st_all[ci, NH + h:NH + h + 1, :] = jnp.sum(w * tst[h], axis=0, keepdims=True)
        st_all[ci, 2 * NH + h:2 * NH + h + 1, :] = jnp.sum(w * dst[h], axis=0, keepdims=True)

    def stat(d, index):
        return remote(st_all.at[index], st_all.at[index], st_send.at[d - 1], st_recv.at[index], peers[d - 1])

    for d in range(1, 8):
        stat(d, ci).start()
    @pl.loop(0, NH)
    def _(h):
        cols = pl.ds(pl.multiple_of(h * HD, HD), HD)
        rows = pl.multiple_of(h * 2 * HD, 2 * HD)
        up_t[pl.ds(rows, HD), :] = upk_ref[:, cols].T
        up_t[pl.ds(rows + HD, HD), :] = upv_ref[:, cols].T

    for d in range(1, 8):
        stat(d, (ci + d) % 8).wait_recv()
    m_all = st_all[0, 0:NH, :]
    for c in range(1, 8):
        m_all = jnp.maximum(m_all, st_all[c, 0:NH, :])
    total = jnp.zeros((NH, NQ), F32)
    product = jnp.zeros((NH, NQ), F32)
    for c in range(8):
        w = jnp.exp2((st_all[c, 0:NH, :] - m_all) * SCALE2)
        total += w * st_all[c, NH:2 * NH, :]
        product += w * st_all[c, 2 * NH:3 * NH, :]
    delta[...] = product / total
    inverse = 1.0 / total
    for h in range(NH):
        wst[h] = jnp.exp2((mst[h] - m_all[h:h + 1]) * SCALE2) * inverse[h:h + 1]

    def up_copy(h, d):
        return remote(
            pbuf.at[h, (ci + d) % 8], rbuf.at[h, d - 1], up_send.at[h, d - 1], up_recv.at[h, d - 1], peers[d - 1]
        )

    def head_tile(h, t):
        rows = pl.ds(pl.multiple_of(t * TILE, TILE), TILE)
        hcols = pl.ds(pl.multiple_of(h * HD, HD), HD)
        kcols = pl.ds(pl.multiple_of(h * 256, 256), 256)
        prob = ebuf[h, rows, :] * wst[h, pl.ds(t, 1), :]
        gs = (prob * (gbuf[h, rows, :] - delta[pl.ds(h, 1), :]) * SCALE).astype(BF16)
        acc[...] += lax.dot_general(gs, kk[rows, kcols], TN, preferred_element_type=F32)
        gk = dot(gs, q_ref[:, hcols]).astype(BF16)
        gv = dot(prob.astype(BF16), go_ref[:, hcols]).astype(BF16)
        kk[rows, kcols] = jnp.concatenate([gk, gv], axis=1)

    def head_sums(h):
        kcols = pl.ds(pl.multiple_of(h * 256, 256), 256)
        gq = acc[:, 0:HD] + acc[:, HD:2 * HD]
        up = dot(lat_t[...], kk[:, kcols]).astype(BF16)
        for c in range(8):
            pbuf[h, c, 0:64, :] = up[c * 64:c * 64 + 64, :]
            pbuf[h, c, 64:80, :] = jnp.concatenate(
                [gq[c * 32:c * 32 + 16], gq[c * 32 + 16:c * 32 + 32]], axis=1
            ).astype(BF16)
        for d in (4, 3, 5, 2, 6, 1, 7):
            up_copy(h, d).start()

    @pl.loop(0, NH - 1)
    def _(h):
        acc[...] = jnp.zeros_like(acc)
        for t in range(8):
            head_tile(h, t)
        head_sums(h)

    sends = ((1, 2), (0, 2), (1, 1), (1, 3), (0, 1), (0, 3), (1, 0), (0, 0))
    mine = pl.ds(pl.multiple_of(core * 128, 128), 128)
    theirs = pl.ds(pl.multiple_of((1 - core) * 128, 128), 128)

    def pairwise(i):
        return remote(gds.at[i], gdr.at[i], gd_send.at[i], gd_recv.at[i], partner)

    def latent_tile(i):
        z_, d = sends[i]
        t = (zh if z_ == 0 else oz) * 4 + ym(d)
        head_tile(NH - 1, t)
        part = dot(kk[pl.ds(pl.multiple_of(t * TILE, TILE), TILE), :], up_t[...])
        lpart[i % 2] = part
        gds[i] = lpart[i % 2, theirs, :].astype(BF16)
        pairwise(i).start()
        held[i] = lpart[i % 2, mine, :]

    def lat_copy(i):
        return remote(ls.at[i], lr.at[i], l_send.at[i], l_recv.at[i], chip(*sends[i]))

    def lat_send(i):
        pairwise(i).wait_recv()
        ls[i] = (held[i] + gdr[i].astype(F32)).astype(BF16)
        lat_copy(i).start()

    acc[...] = jnp.zeros_like(acc)
    for i in range(8):
        latent_tile(i)
        if i >= 2:
            lat_send(i - 2)
    lat_send(6)
    head_sums(NH - 1)
    for h in range(NH):
        for d in range(1, 8):
            up_copy(h, d).wait_recv()
        out = pbuf[h, ci].astype(F32)
        for d in range(7):
            out += rbuf[h, d].astype(F32)
        cols = slice(h * HD, (h + 1) * HD)
        gk_out[:, cols] = out[0:64, 0:HD]
        gv_out[:, cols] = out[0:64, HD:2 * HD]
        gq_out[0:16, cols] = out[64:80, 0:HD]
        gq_out[16:32, cols] = out[64:80, HD:2 * HD]
    pairwise(7).wait_recv()
    out = held[7] + gdr[7].astype(F32)
    for i in range(7):
        lat_copy(i).wait_recv()
        out += lr[i].astype(F32)
    gl_out[...] = out

    ag(0, own_slot, partner).wait_send()
    for k in range(1, 8):
        outgoing(k).wait_send()
        forward(k).wait_send()
    for d in range(1, 8):
        stat(d, ci).wait_send()
        for h in range(NH):
            up_copy(h, d).wait_send()
    for i in range(8):
        pairwise(i).wait_send()
    for i in range(7):
        lat_copy(i).wait_send()


def settle(*refs):
    for source, result in zip(refs[:4], refs[4:]):
        result[...] = source[...]


def local(queries, grad_out, latent, up_key, up_value):
    dma = pltpu.SemaphoreType.DMA
    vmem = pltpu.VMEM
    full = pl.BlockSpec(memory_space=pltpu.VMEM)
    place = pl.BlockSpec(memory_space=pl.ANY)
    shape = jax.ShapeDtypeStruct
    results = (
        shape((32, 1024), F32), shape((128, 512), F32),
        shape((64, 1024), F32), shape((64, 1024), F32),
    )
    sums = pl.pallas_call(
        kernel,
        out_shape=results,
        in_specs=[place] * 5,
        out_specs=(full,) * 4,
        scratch_shapes=[
            vmem((NQ, 1024), BF16), vmem((NQ, 1024), BF16), vmem((512, 1024), BF16), vmem((512, 1024), BF16),
            vmem((ROWS, 512), BF16), vmem((512, ROWS), BF16), vmem((2048, 512), BF16),
            vmem((NH, HD, NQ), BF16), vmem((NH, HD, NQ), BF16),
            vmem((ROWS, 2048), BF16), vmem((NH, ROWS, NQ), F32), vmem((NH, ROWS, NQ), F32),
            vmem((TILE, NQ), F32),
            vmem((NH, 8, NQ), F32), vmem((NH, 8, NQ), F32), vmem((NH, 8, NQ), F32),
            vmem((8, 3 * NH, NQ), F32), vmem((NH, 8, NQ), F32), vmem((NH, NQ), F32),
            vmem((256, 256), F32),
            vmem((NH, 8, 80, 256), BF16), vmem((NH, 7, 80, 256), BF16),
            vmem((8, 128, 512), BF16), vmem((8, 128, 512), BF16), vmem((7, 128, 512), BF16), vmem((7, 128, 512), BF16),
            vmem((8, 128, 512), F32), vmem((2, 256, 512), F32),
            dma((5,)), dma((15,)), dma((16,)), dma((7,)), dma((8,)), dma((NH, 7)), dma((NH, 7)),
            dma((8,)), dma((8,)), dma((7,)), dma((7,)),
        ],
        compiler_params=pltpu.CompilerParams(
            collective_id=0, has_side_effects=True, vmem_limit_bytes=67043328
        ),
    )(queries, grad_out, latent, up_key, up_value)
    return pl.pallas_call(settle, out_shape=results, in_specs=[full] * 4, out_specs=(full,) * 4)(*sums)


def solution(mesh):
    return jax.shard_map(
        local,
        mesh=mesh,
        in_specs=(
            P(None, "head"),
            P(None, "head"),
            P(("ctx", "head"), None),
            P(None, "head"),
            P(None, "head"),
        ),
        out_specs=(P("ctx", "head"), P(("ctx", "head"), None), P("ctx", "head"), P("ctx", "head")),
        check_vma=False,
    )
```

time: 93.2 us -> 71.9 us (0.77)
  Pallas kernels: 87.9 us -> 71.1 us
  local copies, waits for them, and re-layouts: 4.4 us -> 0 us
    pallas_call x1 -> x2, Pallas kernels: 87.9 us -> 71.1 us  [the longest x1 69 us: local(): pl.pallas_call(kernel, out_shape=results, in_specs=[place] * 5, out_specs...]
    unnamed x10 -> x0, local copies, waits for them, and re-layouts: 4.4 us -> none
where the time goes in v2:
time: 71.9 us; the launch traced here: 71.7 us
  Pallas kernels  71.1 us (99%)
    pallas_call x1, Pallas kernels, local(): pl.pallas_call(kernel, out_shape=results, in_specs=[place] * 5, out_specs...  69 us
    pallas_call x1, Pallas kernels, local(): pl.pallas_call(settle, out_shape=results, in_specs=[full] * 4, out_specs=...  2.11 us

profile of v2, /device:TPU:1, one launch (start us, length us, event | category | flops | bytes accessed | tf_op | source)
XLA Modules:
  0.0 71.7 jit_solution(1211219796444444165)
XLA Ops:
  0.6 69.0 %shard_map.84 = (f32[32,1024]{1,0:T(8,128)}, f32[128,512]{1,0:T(8,128)}, f32[64,1024]{1,0:T(8,128)}, f32[64,1024]{1,0:T(8,128)}) custom-call(bf16[256,1024]{1,0:T(8,128)(2,1)} %q_hbm.1, bf16[256,1024]{1,0:T(8,128)(2,1)} %go_hbm.1, bf16[128,512]{1,0:T(8,128)(2,1)} %own_hbm.1, bf16[512,1024]{1,0:T(8,128)(2,1)} %upk_hbm.1, bf16[512,1024]{1,0:T(8,128)(2,1)} %upv_hbm.1), custom_call_target="tpu_custom_call" | custom-call | tf_op jit(solution)/shard_map/pallas_call | solution.py:315
  69.6 2.1 %shard_map.85 = (f32[32,1024]{1,0:T(8,128)}, f32[128,512]{1,0:T(8,128)}, f32[64,1024]{1,0:T(8,128)}, f32[64,1024]{1,0:T(8,128)}) custom-call(f32[32,1024]{1,0:T(8,128)} %get-tuple-element.8.refs_0_, f32[128,512]{1,0:T(8,128)} %get-tuple-element.9.refs_1_, f32[64,1024]{1,0:T(8,128)} %get-tuple-element.10.refs_2_, f32[64,1024]{1,0:T(8,128)} %get-tuple-element.11.refs_3_), custom_call_target="tpu_custom_call" | custom-call | tf_op jit(solution)/shard_map/pallas_call | solution.py:339

commit v3 on v2

--- a/solution.py
+++ b/solution.py
@@ -31,7 +31,7 @@
     q_ref, go_ref, upk_ref, upv_ref,
     lat, lat_t, up_t, q_t, go_t, kk, ebuf, gbuf, bias,
     mst, tst, dst, st_all, wst, delta, acc,
-    pbuf, rbuf, gds, gdr, ls, lr, held, lpart,
+    pbuf, rbuf, gds, gdr, ls, lr,
     in_sem, ag_send, ag_recv, st_send, st_recv, up_send, up_recv,
     gd_send, gd_recv, l_send, l_recv,
 ):
@@ -72,7 +72,7 @@
     for load in loads:
         load.start()
 
-    order = ((1, 0), (0, 3), (0, 1), (1, 3), (1, 1), (0, 2), (1, 2))
+    order = ((1, 0), (0, 3), (0, 1), (1, 3), (0, 2), (1, 1), (1, 2))
     barrier = pltpu.get_barrier_semaphore()
     for d in [partner] + [chip(z_, d) for z_, d in order] + peers:
         pl.semaphore_signal(barrier, inc=1, device_id=d, device_id_type=MESH)
@@ -112,48 +112,48 @@
     key_row = lax.broadcasted_iota(jnp.int32, (TILE, NQ), 0)
     query_col = lax.broadcasted_iota(jnp.int32, (TILE, NQ), 1)
 
-    @pl.loop(0, 8)
-    def _(step):
-        @pl.when(step == 1)
-        def _():
-            outgoing(4).start()
-            outgoing(5).start()
-
-        for k in range(1, 8):
-            @pl.when(step == max(k - 1, 1))
-            def _(k=k):
-                ag(k, slots[k], partner).wait_recv()
-                forward(k).start()
-                if k == 1:
-                    outgoing(6).start()
-                    outgoing(7).start()
-        for k in range(8):
-            @pl.when(step == k)
-            def _(k=k):
-                ag(0, slots[k] + 1 - 2 * core, partner).wait_recv()
-        y_t = (y + jnp.where(step < 2, 0, jnp.where(step >= 6, 2, jnp.where(step % 2 == 0, 3, 1)))) % 4
-        z_t = (zh + jnp.where(step < 4, jnp.where(step == 1, 1, 0), jnp.where(step == 6, 0, 1))) % 2
+    def receive(k):
+        ag(k, slots[k], partner).wait_recv()
+        forward(k).start()
+
+    def from_partner(k):
+        ag(0, slots[k] + 1 - 2 * core, partner).wait_recv()
+
+    def score_tile(step, base, pairs):
+        odd = step % 2
+        y_t = (y + jnp.where(step < 2, 0, jnp.where(step < 5, 3 - 2 * odd, 1 + odd))) % 4
+        z_t = (zh + jnp.where(step < 4, jnp.where(step == 1, 1, 0), jnp.where(step == 5, 0, 1))) % 2
         t = z_t * 4 + y_t
         rows = pl.ds(pl.multiple_of(t * TILE, TILE), TILE)
         limit = jnp.where(jnp.logical_and(last_owner, t == 7), 0, 4 * TILE)
         bias[...] = jnp.where(key_row > query_col + limit, NEG, 0.0)
         block = lat[rows, :]
         lat_t[:, rows] = block.T
-        for pair in range(NH // 2):
-            cols = slice(pair * 2 * HD, (pair + 1) * 2 * HD)
+
+        def project(pair):
+            first = base + pair * 2
+            cols = pl.ds(first * HD, 2 * HD) if isinstance(first, int) else pl.ds(pl.multiple_of(first * HD, 2 * HD), 2 * HD)
             k2 = dot(block, upk_ref[:, cols])
             v2 = dot(block, upv_ref[:, cols]).astype(BF16)
+            parts = []
             for b in range(2):
-                h = pair * 2 + b
                 half = slice(b * HD, (b + 1) * HD)
                 key = k2[:, half]
                 key_hi = key.astype(BF16)
                 key_lo = (key - key_hi.astype(F32)).astype(BF16)
                 both = jnp.concatenate([key_hi, key_lo], axis=1)
-                kk[rows, h * 256:(h + 1) * 256] = both
+                start = (first + b) * 256
+                kcols = pl.ds(start, 256) if isinstance(start, int) else pl.ds(pl.multiple_of(start, 256), 256)
+                kk[rows, kcols] = both
+                parts.append((both, v2[:, half]))
+            return parts
+
+        def score(pair, parts):
+            for b in range(2):
+                h = base + pair * 2 + b
                 qt = q_t[h]
-                s = dot(both, jnp.concatenate([qt, qt], axis=0)) + bias[...]
-                g = dot(v2[:, half], go_t[h])
+                s = dot(parts[b][0], jnp.concatenate([qt, qt], axis=0)) + bias[...]
+                g = dot(parts[b][1], go_t[h])
                 m = jnp.max(s, axis=0, keepdims=True)
                 e = jnp.exp2((s - m) * SCALE2)
                 ebuf[h, rows, :] = e
@@ -162,19 +162,67 @@
                 tst[h, pl.ds(t, 1), :] = jnp.sum(e, axis=0, keepdims=True)
                 dst[h, pl.ds(t, 1), :] = jnp.sum(e * g, axis=0, keepdims=True)
 
-    for h in range(NH):
-        mt = mst[h]
-        m = jnp.max(mt, axis=0, keepdims=True)
-        w = jnp.exp2((mt - m) * SCALE2)
-        st_all[ci, h:h + 1, :] = m
-        st_all[ci, NH + h:NH + h + 1, :] = jnp.sum(w * tst[h], axis=0, keepdims=True)
-        st_all[ci, 2 * NH + h:2 * NH + h + 1, :] = jnp.sum(w * dst[h], axis=0, keepdims=True)
-
-    def stat(d, index):
-        return remote(st_all.at[index], st_all.at[index], st_send.at[d - 1], st_recv.at[index], peers[d - 1])
-
-    for d in range(1, 8):
-        stat(d, ci).start()
+        pending = project(0)
+        for pair in range(pairs):
+            following = project(pair + 1) if pair + 1 < pairs else None
+            score(pair, pending)
+            pending = following
+
+    def stat(g, d, index):
+        place = st_all.at[g, index]
+        return remote(place, place, st_send.at[g, d - 1], st_recv.at[g, index], peers[d - 1])
+
+    def stats_send(g):
+        for i in range(NH):
+            h = g * NH + i
+            mt = mst[h]
+            m = jnp.max(mt, axis=0, keepdims=True)
+            w = jnp.exp2((mt - m) * SCALE2)
+            st_all[g, ci, i:i + 1, :] = m
+            st_all[g, ci, NH + i:NH + i + 1, :] = jnp.sum(w * tst[h], axis=0, keepdims=True)
+            st_all[g, ci, 2 * NH + i:2 * NH + i + 1, :] = jnp.sum(w * dst[h], axis=0, keepdims=True)
+        for d in range(1, 8):
+            stat(g, d, ci).start()
+
+    def stats_join(g):
+        for d in range(1, 8):
+            stat(g, d, (ci + d) % 8).wait_recv()
+        half = NH
+        m_all = st_all[g, 0, 0:half, :]
+        for c in range(1, 8):
+            m_all = jnp.maximum(m_all, st_all[g, c, 0:half, :])
+        total = jnp.zeros((half, NQ), F32)
+        product = jnp.zeros((half, NQ), F32)
+        for c in range(8):
+            w = jnp.exp2((st_all[g, c, 0:half, :] - m_all) * SCALE2)
+            total += w * st_all[g, c, NH:NH + half, :]
+            product += w * st_all[g, c, 2 * NH:2 * NH + half, :]
+        delta[g * half:(g + 1) * half, :] = product / total
+        inverse = 1.0 / total
+        for i in range(half):
+            h = g * half + i
+            wst[h] = jnp.exp2((mst[h] - m_all[i:i + 1]) * SCALE2) * inverse[i:i + 1]
+
+    @pl.loop(0, 8)
+    def _(step):
+        for k in range(1, 8):
+            @pl.when(step == max(k - 1, 1))
+            def _(k=k):
+                if k == 1:
+                    outgoing(4).start()
+                    outgoing(5).start()
+                receive(k)
+                if k == 1:
+                    outgoing(6).start()
+                    outgoing(7).start()
+        for k in range(8):
+            @pl.when(step == k)
+            def _(k=k):
+                from_partner(k)
+        score_tile(step, 0, NH // 2)
+
+    stats_send(0)
+
     @pl.loop(0, NH)
     def _(h):
         cols = pl.ds(pl.multiple_of(h * HD, HD), HD)
@@ -182,26 +230,66 @@
         up_t[pl.ds(rows, HD), :] = upk_ref[:, cols].T
         up_t[pl.ds(rows + HD, HD), :] = upv_ref[:, cols].T
 
-    for d in range(1, 8):
-        stat(d, (ci + d) % 8).wait_recv()
-    m_all = st_all[0, 0:NH, :]
-    for c in range(1, 8):
-        m_all = jnp.maximum(m_all, st_all[c, 0:NH, :])
-    total = jnp.zeros((NH, NQ), F32)
-    product = jnp.zeros((NH, NQ), F32)
-    for c in range(8):
-        w = jnp.exp2((st_all[c, 0:NH, :] - m_all) * SCALE2)
-        total += w * st_all[c, NH:2 * NH, :]
-        product += w * st_all[c, 2 * NH:3 * NH, :]
-    delta[...] = product / total
-    inverse = 1.0 / total
-    for h in range(NH):
-        wst[h] = jnp.exp2((mst[h] - m_all[h:h + 1]) * SCALE2) * inverse[h:h + 1]
-
-    def up_copy(h, d):
-        return remote(
-            pbuf.at[h, (ci + d) % 8], rbuf.at[h, d - 1], up_send.at[h, d - 1], up_recv.at[h, d - 1], peers[d - 1]
-        )
+    stats_join(0)
+
+    zpeer = (x * 2 + 1 - zl, hi)
+    kinds = (0, 1, 0, 1, 0, 1, 2, 2)
+    straight = ((2, 1), (2, 0), (1, 1), (3, 1), (1, 0), (3, 0), (0, 1))
+
+    def up_copy(h, j, src, dst, device):
+        return remote(src, dst, up_send.at[h, j], up_recv.at[h, j], device)
+
+    def first_copies(kind, h):
+        if kind == 0:
+            return [
+                up_copy(h, d - 1, pbuf.at[h, xm(d)], rbuf.at[h, pl.ds(2 * d - 2, 2)], (xm(d) * 2 + zl, hi))
+                for d in (2, 1, 3)
+            ]
+        if kind == 1:
+            return [up_copy(h, 0, pbuf.at[h, :, 1 - zl], rbuf.at[h, pl.ds(0, 4)], zpeer)]
+        return [
+            up_copy(h, j, pbuf.at[h, xm(d), (zl + z_) % 2], rbuf.at[h, j], (xm(d) * 2 + (zl + z_) % 2, hi))
+            for j, (d, z_) in enumerate(straight)
+        ]
+
+    def second_copies(kind, h):
+        if kind == 0:
+            return [up_copy(h, 3, pbuf.at[h, x, 1 - zl], rbuf.at[h, 6], zpeer)]
+        if kind == 1:
+            return [
+                up_copy(h, d, pbuf.at[h, xm(d), zl], rbuf.at[h, 3 + d], (xm(d) * 2 + zl, hi)) for d in (2, 1, 3)
+            ]
+        return []
+
+    def pass_on(h):
+        kind = kinds[h]
+        for copy in first_copies(kind, h):
+            copy.wait_recv()
+        if kind == 0:
+            part = pbuf[h, x, 1 - zl].astype(F32)
+            for d in range(3):
+                part += rbuf[h, 2 * d + 1 - zl].astype(F32)
+            pbuf[h, x, 1 - zl] = part.astype(BF16)
+        else:
+            for d in range(1, 4):
+                pbuf[h, xm(d), zl] = (pbuf[h, xm(d), zl].astype(F32) + rbuf[h, xm(d)].astype(F32)).astype(BF16)
+        for copy in second_copies(kind, h):
+            copy.start()
+
+    def up_result(h):
+        kind = kinds[h]
+        for copy in second_copies(kind, h) if kind < 2 else first_copies(kind, h):
+            copy.wait_recv()
+        out = pbuf[h, x, zl].astype(F32)
+        if kind == 0:
+            pieces = [2 * d + zl for d in range(3)] + [6]
+        elif kind == 1:
+            pieces = [x, 4, 5, 6]
+        else:
+            pieces = list(range(7))
+        for piece in pieces:
+            out += rbuf[h, piece].astype(F32)
+        return out
 
     def head_tile(h, t):
         rows = pl.ds(pl.multiple_of(t * TILE, TILE), TILE)
@@ -219,12 +307,14 @@
         gq = acc[:, 0:HD] + acc[:, HD:2 * HD]
         up = dot(lat_t[...], kk[:, kcols]).astype(BF16)
         for c in range(8):
-            pbuf[h, c, 0:64, :] = up[c * 64:c * 64 + 64, :]
-            pbuf[h, c, 64:80, :] = jnp.concatenate(
+            pbuf[h, c // 2, c % 2, 0:64, :] = up[c * 64:c * 64 + 64, :]
+            pbuf[h, c // 2, c % 2, 64:80, :] = jnp.concatenate(
                 [gq[c * 32:c * 32 + 16], gq[c * 32 + 16:c * 32 + 32]], axis=1
             ).astype(BF16)
-        for d in (4, 3, 5, 2, 6, 1, 7):
-            up_copy(h, d).start()
+
+    def launch(kind, h):
+        for copy in first_copies(kind, h):
+            copy.start()
 
     @pl.loop(0, NH - 1)
     def _(h):
@@ -233,9 +323,24 @@
             head_tile(h, t)
         head_sums(h)
 
+        @pl.when(jnp.logical_and(h < 6, h % 2 == 0))
+        def _():
+            launch(0, h)
+
+        @pl.when(jnp.logical_and(h < 6, h % 2 == 1))
+        def _():
+            launch(1, h)
+
+        @pl.when(h == 5)
+        def _():
+            pass_on(0)
+
+        @pl.when(h == 6)
+        def _():
+            launch(2, h)
+            pass_on(1)
+
     sends = ((1, 2), (0, 2), (1, 1), (1, 3), (0, 1), (0, 3), (1, 0), (0, 0))
-    mine = pl.ds(pl.multiple_of(core * 128, 128), 128)
-    theirs = pl.ds(pl.multiple_of((1 - core) * 128, 128), 128)
 
     def pairwise(i):
         return remote(gds.at[i], gdr.at[i], gd_send.at[i], gd_recv.at[i], partner)
@@ -243,54 +348,64 @@
     def latent_tile(i):
         z_, d = sends[i]
         t = (zh if z_ == 0 else oz) * 4 + ym(d)
-        head_tile(NH - 1, t)
         part = dot(kk[pl.ds(pl.multiple_of(t * TILE, TILE), TILE), :], up_t[...])
-        lpart[i % 2] = part
-        gds[i] = lpart[i % 2, theirs, :].astype(BF16)
+        for b in range(2):
+            cols = slice(b * 256, (b + 1) * 256)
+            ebuf[i, b * 256:(b + 1) * 256, :] = part[:, cols]
+            gds[i, :, cols] = ebuf[i, pl.ds(pl.multiple_of(b * 256 + (1 - core) * 128, 128), 128), :].astype(BF16)
         pairwise(i).start()
-        held[i] = lpart[i % 2, mine, :]
+
+    def held(i, b):
+        rows = pl.ds(pl.multiple_of(b * 256 + core * 128, 128), 128)
+        return ebuf[i, rows, :] + gdr[i, :, b * 256:(b + 1) * 256].astype(F32)
 
     def lat_copy(i):
         return remote(ls.at[i], lr.at[i], l_send.at[i], l_recv.at[i], chip(*sends[i]))
 
     def lat_send(i):
         pairwise(i).wait_recv()
-        ls[i] = (held[i] + gdr[i].astype(F32)).astype(BF16)
+        for b in range(2):
+            ls[i, :, b * 256:(b + 1) * 256] = held(i, b).astype(BF16)
         lat_copy(i).start()
 
     acc[...] = jnp.zeros_like(acc)
+    for t in range(8):
+        head_tile(NH - 1, t)
     for i in range(8):
         latent_tile(i)
         if i >= 2:
             lat_send(i - 2)
+        if i == 3:
+            head_sums(NH - 1)
+            launch(2, NH - 1)
+        if i % 2 == 0:
+            pass_on(2 + i // 2)
     lat_send(6)
-    head_sums(NH - 1)
     for h in range(NH):
-        for d in range(1, 8):
-            up_copy(h, d).wait_recv()
-        out = pbuf[h, ci].astype(F32)
-        for d in range(7):
-            out += rbuf[h, d].astype(F32)
+        out = up_result(h)
         cols = slice(h * HD, (h + 1) * HD)
         gk_out[:, cols] = out[0:64, 0:HD]
         gv_out[:, cols] = out[0:64, HD:2 * HD]
         gq_out[0:16, cols] = out[64:80, 0:HD]
         gq_out[16:32, cols] = out[64:80, HD:2 * HD]
     pairwise(7).wait_recv()
-    out = held[7] + gdr[7].astype(F32)
     for i in range(7):
         lat_copy(i).wait_recv()
-        out += lr[i].astype(F32)
-    gl_out[...] = out
+    for b in range(2):
+        out = held(7, b)
+        for i in range(7):
+            out += lr[i, :, b * 256:(b + 1) * 256].astype(F32)
+        gl_out[:, b * 256:(b + 1) * 256] = out
 
     ag(0, own_slot, partner).wait_send()
     for k in range(1, 8):
         outgoing(k).wait_send()
         forward(k).wait_send()
     for d in range(1, 8):
-        stat(d, ci).wait_send()
-        for h in range(NH):
-            up_copy(h, d).wait_send()
+        stat(0, d, ci).wait_send()
+    for h in range(NH):
+        for copy in first_copies(kinds[h], h) + second_copies(kinds[h], h):
+            copy.wait_send()
     for i in range(8):
         pairwise(i).wait_send()
     for i in range(7):
@@ -324,12 +439,11 @@
             vmem((ROWS, 2048), BF16), vmem((NH, ROWS, NQ), F32), vmem((NH, ROWS, NQ), F32),
             vmem((TILE, NQ), F32),
             vmem((NH, 8, NQ), F32), vmem((NH, 8, NQ), F32), vmem((NH, 8, NQ), F32),
-            vmem((8, 3 * NH, NQ), F32), vmem((NH, 8, NQ), F32), vmem((NH, NQ), F32),
+            vmem((1, 8, 3 * NH, NQ), F32), vmem((NH, 8, NQ), F32), vmem((NH, NQ), F32),
             vmem((256, 256), F32),
-            vmem((NH, 8, 80, 256), BF16), vmem((NH, 7, 80, 256), BF16),
+            vmem((NH, 4, 2, 80, 256), BF16), vmem((NH, 7, 80, 256), BF16),
             vmem((8, 128, 512), BF16), vmem((8, 128, 512), BF16), vmem((7, 128, 512), BF16), vmem((7, 128, 512), BF16),
-            vmem((8, 128, 512), F32), vmem((2, 256, 512), F32),
-            dma((5,)), dma((15,)), dma((16,)), dma((7,)), dma((8,)), dma((NH, 7)), dma((NH, 7)),
+            dma((5,)), dma((15,)), dma((16,)), dma((1, 7)), dma((1, 8)), dma((NH, 7)), dma((NH, 7)),
             dma((8,)), dma((8,)), dma((7,)), dma((7,)),
         ],
         compiler_params=pltpu.CompilerParams(

time: 71.9 us -> 69.4 us (0.965)
  Pallas kernels: 71.1 us -> 68.7 us
    pallas_call x1, Pallas kernels: 69 us -> 66.6 us  [local(): pl.pallas_call(kernel, out_shape=results, in_specs=[place] * 5, out_specs...]
where the time goes in v3:
time: 69.4 us; the launch traced here: 69.3 us
  Pallas kernels  68.7 us (99%)
    pallas_call x1, Pallas kernels, local(): pl.pallas_call(kernel, out_shape=results, in_specs=[place] * 5, out_specs...  66.6 us
    pallas_call x1, Pallas kernels, local(): pl.pallas_call(settle, out_shape=results, in_specs=[full] * 4, out_specs=...  2.11 us

profile of v3, /device:TPU:1, one launch (start us, length us, event | category | flops | bytes accessed | tf_op | source)
XLA Modules:
  0.0 69.3 jit_solution(7941051264521976621)
XLA Ops:
  0.6 66.6 %shard_map.84 = (f32[32,1024]{1,0:T(8,128)}, f32[128,512]{1,0:T(8,128)}, f32[64,1024]{1,0:T(8,128)}, f32[64,1024]{1,0:T(8,128)}) custom-call(bf16[256,1024]{1,0:T(8,128)(2,1)} %q_hbm.1, bf16[256,1024]{1,0:T(8,128)(2,1)} %go_hbm.1, bf16[128,512]{1,0:T(8,128)(2,1)} %own_hbm.1, bf16[512,1024]{1,0:T(8,128)(2,1)} %upk_hbm.1, bf16[512,1024]{1,0:T(8,128)(2,1)} %upv_hbm.1), custom_call_target="tpu_custom_call" | custom-call | tf_op jit(solution)/shard_map/pallas_call | solution.py:430
  67.2 2.1 %shard_map.85 = (f32[32,1024]{1,0:T(8,128)}, f32[128,512]{1,0:T(8,128)}, f32[64,1024]{1,0:T(8,128)}, f32[64,1024]{1,0:T(8,128)}) custom-call(f32[32,1024]{1,0:T(8,128)} %get-tuple-element.8.refs_0_, f32[128,512]{1,0:T(8,128)} %get-tuple-element.9.refs_1_, f32[64,1024]{1,0:T(8,128)} %get-tuple-element.10.refs_2_, f32[64,1024]{1,0:T(8,128)} %get-tuple-element.11.refs_3_), custom_call_target="tpu_custom_call" | custom-call | tf_op jit(solution)/shard_map/pallas_call | solution.py:453

commit v4 on v3

--- a/solution.py
+++ b/solution.py
@@ -27,7 +27,8 @@
 
 def kernel(
     q_hbm, go_hbm, own_hbm, upk_hbm, upv_hbm,
-    gq_out, gl_out, gk_out, gv_out,
+    gq_hbm, gl_hbm, gk_hbm, gv_hbm,
+    gq_out, gl_out, gk_out, gv_out, out_sem,
     q_ref, go_ref, upk_ref, upv_ref,
     lat, lat_t, up_t, q_t, go_t, kk, ebuf, gbuf, bias,
     mst, tst, dst, st_all, wst, delta, acc,
@@ -340,14 +341,17 @@
             launch(2, h)
             pass_on(1)
 
-    sends = ((1, 2), (0, 2), (1, 1), (1, 3), (0, 1), (0, 3), (1, 0), (0, 0))
+    sends = ((1, 1), (1, 3), (1, 2), (1, 0), (0, 2), (0, 1), (0, 3), (0, 0))
 
     def pairwise(i):
         return remote(gds.at[i], gdr.at[i], gd_send.at[i], gd_recv.at[i], partner)
 
+    def tile_of(i):
+        z_, d = sends[i]
+        return (zh if z_ == 0 else oz) * 4 + ym(d)
+
     def latent_tile(i):
-        z_, d = sends[i]
-        t = (zh if z_ == 0 else oz) * 4 + ym(d)
+        t = tile_of(i)
         part = dot(kk[pl.ds(pl.multiple_of(t * TILE, TILE), TILE), :], up_t[...])
         for b in range(2):
             cols = slice(b * 256, (b + 1) * 256)
@@ -369,16 +373,20 @@
         lat_copy(i).start()
 
     acc[...] = jnp.zeros_like(acc)
-    for t in range(8):
-        head_tile(NH - 1, t)
-    for i in range(8):
+    head_tile(NH - 1, tile_of(0))
+    latent_tile(0)
+    for i in range(1, 8):
+        head_tile(NH - 1, tile_of(i))
+    for i in range(1, 8):
         latent_tile(i)
-        if i >= 2:
+        if i == 1:
+            lat_send(0)
+        if i >= 3:
             lat_send(i - 2)
         if i == 3:
             head_sums(NH - 1)
             launch(2, NH - 1)
-        if i % 2 == 0:
+        if i % 2 == 1:
             pass_on(2 + i // 2)
     lat_send(6)
     for h in range(NH):
@@ -388,6 +396,12 @@
         gv_out[:, cols] = out[0:64, HD:2 * HD]
         gq_out[0:16, cols] = out[64:80, 0:HD]
         gq_out[16:32, cols] = out[64:80, HD:2 * HD]
+    leaving = [
+        pltpu.make_async_copy(src, dst, out_sem.at[i])
+        for i, (src, dst) in enumerate(((gq_out, gq_hbm), (gk_out, gk_hbm), (gv_out, gv_hbm), (gl_out, gl_hbm)))
+    ]
+    for copy in leaving[:3]:
+        copy.start()
     pairwise(7).wait_recv()
     for i in range(7):
         lat_copy(i).wait_recv()
@@ -397,6 +411,10 @@
             out += lr[i, :, b * 256:(b + 1) * 256].astype(F32)
         gl_out[:, b * 256:(b + 1) * 256] = out
 
+    leaving[3].start()
+
+    for copy in leaving:
+        copy.wait()
     ag(0, own_slot, partner).wait_send()
     for k in range(1, 8):
         outgoing(k).wait_send()
@@ -413,14 +431,22 @@
 
 
 def settle(*refs):
-    for source, result in zip(refs[:4], refs[4:]):
-        result[...] = source[...]
+    sources, results, buffers = refs[:4], refs[4:8], refs[8:12]
+    in_sem, out_sem = refs[12:]
+    loads = [pltpu.make_async_copy(sources[i], buffers[i], in_sem.at[i]) for i in range(4)]
+    stores = [pltpu.make_async_copy(buffers[i], results[i], out_sem.at[i]) for i in range(4)]
+    for load in loads:
+        load.start()
+    for load, store in zip(loads, stores):
+        load.wait()
+        store.start()
+    for store in stores:
+        store.wait()
 
 
 def local(queries, grad_out, latent, up_key, up_value):
     dma = pltpu.SemaphoreType.DMA
     vmem = pltpu.VMEM
-    full = pl.BlockSpec(memory_space=pltpu.VMEM)
     place = pl.BlockSpec(memory_space=pl.ANY)
     shape = jax.ShapeDtypeStruct
     results = (
@@ -431,8 +457,9 @@
         kernel,
         out_shape=results,
         in_specs=[place] * 5,
-        out_specs=(full,) * 4,
+        out_specs=(place,) * 4,
         scratch_shapes=[
+            *(vmem(r.shape, F32) for r in results), dma((4,)),
             vmem((NQ, 1024), BF16), vmem((NQ, 1024), BF16), vmem((512, 1024), BF16), vmem((512, 1024), BF16),
             vmem((ROWS, 512), BF16), vmem((512, ROWS), BF16), vmem((2048, 512), BF16),
             vmem((NH, HD, NQ), BF16), vmem((NH, HD, NQ), BF16),
@@ -450,7 +477,13 @@
             collective_id=0, has_side_effects=True, vmem_limit_bytes=67043328
         ),
     )(queries, grad_out, latent, up_key, up_value)
-    return pl.pallas_call(settle, out_shape=results, in_specs=[full] * 4, out_specs=(full,) * 4)(*sums)
+    return pl.pallas_call(
+        settle,
+        out_shape=results,
+        in_specs=[place] * 4,
+        out_specs=(place,) * 4,
+        scratch_shapes=[*(vmem(r.shape, F32) for r in results), dma((4,)), dma((4,))],
+    )(*sums)
 
 
 def solution(mesh):

time: 69.4 us -> 67.5 us (0.973)
  Pallas kernels: 68.7 us -> 66.7 us
    pallas_call x1, Pallas kernels: 66.6 us -> 64.8 us  [local(): pl.pallas_call(kernel, out_shape=results, in_specs=[place] * 5, out_specs...]
where the time goes in v4:
time: 67.5 us; the launch traced here: 67.4 us
  Pallas kernels  66.7 us (99%)
    pallas_call x1, Pallas kernels, local(): pl.pallas_call(kernel, out_shape=results, in_specs=[place] * 5, out_specs...  64.8 us
    pallas_call x1, Pallas kernels, local(): pl.pallas_call(settle, out_shape=results, in_specs=[place] * 4, out_specs...  1.97 us

profile of v4, /device:TPU:1, one launch (start us, length us, event | category | flops | bytes accessed | tf_op | source)
XLA Modules:
  0.0 67.4 jit_solution(391866080970007106)
XLA Ops:
  0.6 64.8 %shard_map.84 = (f32[32,1024]{1,0:T(8,128)}, f32[128,512]{1,0:T(8,128)}, f32[64,1024]{1,0:T(8,128)}, f32[64,1024]{1,0:T(8,128)}) custom-call(bf16[256,1024]{1,0:T(8,128)(2,1)} %q_hbm.1, bf16[256,1024]{1,0:T(8,128)(2,1)} %go_hbm.1, bf16[128,512]{1,0:T(8,128)(2,1)} %own_hbm.1, bf16[512,1024]{1,0:T(8,128)(2,1)} %upk_hbm.1, bf16[512,1024]{1,0:T(8,128)(2,1)} %upv_hbm.1), custom_call_target="tpu_custom_call" | custom-call | tf_op jit(solution)/shard_map/pallas_call | solution.py:456
  65.4 2.0 %shard_map.85 = (f32[32,1024]{1,0:T(8,128)}, f32[128,512]{1,0:T(8,128)}, f32[64,1024]{1,0:T(8,128)}, f32[64,1024]{1,0:T(8,128)}) custom-call(f32[32,1024]{1,0:T(8,128)} %get-tuple-element.8.refs_0_, f32[128,512]{1,0:T(8,128)} %get-tuple-element.9.refs_1_, f32[64,1024]{1,0:T(8,128)} %get-tuple-element.10.refs_2_, f32[64,1024]{1,0:T(8,128)} %get-tuple-element.11.refs_3_), custom_call_target="tpu_custom_call" | custom-call | tf_op jit(solution)/shard_map/pallas_call | solution.py:480
